TPU v7x, 512 devices: a whole 4x8x8 slice. The times are simulated.
512 devices in a mesh: row: 32 (over y, z_hi, core), col: 16 (over x, z_lo).
Axes of the slice: x: 4, y: 8, z: 8 (z_hi: 2, z_lo: 4; z = z_hi * 4 + z_lo), core: 2. Of those that a mesh axis runs over, the one named last changes fastest.
Arguments:
- traces: bfloat16 [2048, 64, 512], P(('row', 'col')), may hold values from -6 to 6
- live_flags: int32 [2048], P(('row', 'col')), may hold values 0 or 1
Outputs:
- correlations: bfloat16 [2048, 2048, 128], P('row', 'col')
Inputs may be any that keep to these rules, and one draw needn't show every extreme that they name: `live_flags`: 1 marks a working channel.
All inputs are finite; a program needn't handle non-finite values. No bound on the sum of `live_flags` on one device may be relied on, other than what follows from the above.
Results may differ from a plain program's by a relative error of at most 0.0058.
Values may be sent and summed in bfloat16 or wider, within the bound.
No kernel may reach another device: no remote copies, remote signals or barrier semaphores. Data moves between devices by JAX's collectives and lax.ppermute only.
A program may use at most 64 MiB of HBM per device.

v0:
```python
import math
import jax
import jax.numpy as jnp
from jax import lax
from jax.sharding import PartitionSpec as P

F = 256
LAGS = 128
SAMP = 512
NW = 64


def make_tables():
    samples = jnp.arange(SAMP, dtype=jnp.int32)
    bins = jnp.arange(F, dtype=jnp.int32)
    phase = samples[:, None] * bins[None, :] % SAMP
    angle = 2.0 * math.pi * phase.astype(jnp.float32) / SAMP
    forward = jnp.concatenate([jnp.cos(angle), -jnp.sin(angle)], axis=1)
    taper = 0.5 - 0.5 * jnp.cos(2.0 * math.pi * samples.astype(jnp.float32) / SAMP)
    near = (jnp.abs(bins[:, None] - bins[None, :]) <= 4).astype(jnp.float32)
    counts = jnp.sum(near, axis=0)
    lagval = jnp.arange(LAGS, dtype=jnp.int32) - LAGS // 2
    lphase = bins[:, None] * lagval[None, :] % SAMP
    langle = 2.0 * math.pi * lphase.astype(jnp.float32) / SAMP
    inverse = jnp.concatenate([jnp.cos(langle), -jnp.sin(langle)], axis=0).astype(jnp.bfloat16)
    return (forward, taper, near, counts, inverse)


def whiten(traces, live_flags, forward, taper, near, counts):
    chans = traces.shape[0]
    tapered = traces.astype(jnp.float32) * taper
    spectra = jnp.dot(tapered.reshape(-1, SAMP), forward, precision=lax.Precision.HIGHEST)
    real_part = spectra[:, :F]
    imag_part = spectra[:, F:]
    power = real_part * real_part + imag_part * imag_part
    smooth = jnp.dot(power, near, precision=lax.Precision.HIGHEST) / counts
    level = jnp.mean(power, axis=1, keepdims=True)
    scale = 1.0 / jnp.sqrt(smooth + 0.05 * level + 1e-06)
    alive = jnp.repeat(live_flags.astype(jnp.float32), NW)[:, None]
    white = jnp.concatenate([real_part * scale, imag_part * scale], axis=1) * alive
    white = white.reshape(chans, NW, 2, F)
    white = jnp.transpose(white, (3, 0, 2, 1)).reshape(F, chans, 2 * NW)
    return white.astype(jnp.bfloat16)


def cross_terms(first, second):
    half = first.shape[-1] // 2
    turned = jnp.concatenate([first[..., half:], -first[..., :half]], axis=2)
    cross_re = jnp.einsum("fik,fjk->fij", first, second, preferred_element_type=jnp.float32)
    cross_im = jnp.einsum("fik,fjk->fij", turned, second, preferred_element_type=jnp.float32)
    return (cross_re, cross_im)


def lag_block(cross_re, cross_im, inverse, low, high):
    stacked = (jnp.concatenate([cross_re, cross_im], axis=0) / math.sqrt(NW)).astype(jnp.bfloat16)
    table = jnp.concatenate([inverse[low:high], inverse[F + low : F + high]], axis=0)
    return lax.dot_general(
        stacked, table, (((0,), (0,)), ((), ())), preferred_element_type=jnp.float32
    )


def on_device(traces, live_flags):
    forward, taper, near, counts, inverse = make_tables()
    white = whiten(traces, live_flags, forward, taper, near, counts)
    per_dev = white.shape[1]
    width = F // 4
    first = lax.all_gather(white, "col", axis=1, tiled=True)
    second = lax.all_gather(white, "row", axis=1, tiled=True)
    pairs = (first, second)
    rows = pairs[0].shape[1]
    cols = pairs[1].shape[1]
    corr = jnp.zeros((rows, cols, LAGS), jnp.float32)
    for block in range(4):
        low = block * width
        high = low + width
        cross_re = None
        cross_im = None
        first, second = pairs
        part_re, part_im = cross_terms(first[low:high], second[low:high])
        cross_re = part_re
        cross_im = part_im
        corr = corr + lag_block(cross_re, cross_im, inverse, low, high)
    corr = corr / math.sqrt(F)
    n_col = lax.axis_size("col")
    chan_i = lax.axis_index("row") * rows + jnp.arange(rows, dtype=jnp.int32)
    local_j = jnp.arange(cols, dtype=jnp.int32)
    chan_j = (local_j // per_dev * n_col + lax.axis_index("col")) * per_dev + local_j % per_dev
    same = chan_i[:, None] == chan_j[None, :]
    corr = jnp.where(same[:, :, None], 0.0, corr)
    return corr.astype(jnp.bfloat16)


def solution(mesh):
    in_specs = (P(("row", "col"), None, None), P(("row", "col")))
    out_specs = P("row", "col", None)
    return jax.shard_map(
        on_device, mesh=mesh, in_specs=in_specs, out_specs=out_specs, check_vma=False
    )
```

profile of v0, /device:TPU:1, one launch (start us, length us, event | category | flops | bytes accessed | tf_op | source)
XLA Modules:
  0.0 307.1 jit_solution(10770554908488322001)
XLA Ops:
  6.6 2.1 sine_negate_fusion
  8.7 1.0 convert_multiply_fusion
  9.7 1.1 fusion.30
  11.8 0.8 copy.32
  14.1 108.5 %all-gather.3.cloned.1.call-done = bf16[256,64,128]{2,0,1:T(8,128)(2,1)} async-done(((bf16[256,4,128]{2,0,1:T(8,128)(2,1)}), bf16[256,64,128]{2,0,1:T(8,128)(2,1)}) %all-gather.3.cloned.1.call-update) | async-done | bytes 4194320 | tf_op jit(solution)/shard_map/all_gather | solution.py:67
  122.6 4.4 %fusion.90 = (bf16[64,64,64]{2,0,1:T(8,128)(2,1)S(1)}, bf16[64,64,64]{2,0,1:T(8,128)(2,1)S(1)}, bf16[64,64,64]{2,0,1:T(8,128)(2,1)S(1)}, bf16[64,64,64]{2,0,1:T(...) fusion(bf16[256,64,128]{2,0,1:T(8,128)(2,1)} %all-gather.3.clon, ...), kind=kLoop, calls=%fused_computation.131 | loop fusion | bytes 8388608 | tf_op jit(solution)/shard_map/slice | solution.py:48
  127.0 1.7 copy.65
  128.6 1.7 copy.57
  130.3 0.7 copy.61
  131.0 0.7 copy.69
  131.7 1.8 copy_negate_fusion.1
  133.4 1.8 copy_negate_fusion.3
  135.2 1.8 copy_negate_fusion.2
  137.0 0.8 copy_negate_fusion
  137.9 2.7 fusion.89
  140.6 117.0 %all-gather.5.cloned.1.call-done = bf16[256,128,128]{2,0,1:T(8,128)(2,1)} async-done(((bf16[256,4,128]{2,0,1:T(8,128)(2,1)}), bf16[256,128,128]{2,0,1:T(8,128)(2,1)}) %all-gather.5.cloned.1.call-update) | async-done | bytes 8388624 | tf_op jit(solution)/shard_map/all_gather | solution.py:68
  257.6 4.7 %fusion.88 = (bf16[64,128,128]{2,0,1:T(8,128)(2,1)S(1)}, bf16[64,128,128]{2,0,1:T(8,128)(2,1)S(1)}, bf16[64,128,128]{2,0,1:T(8,128)(2,1)S(1)}, bf16[64,128,128]{2,0,1:T(8,128)(2,1)S(1)}) fusion(bf16[256,128,128]{2,0,1:T(8,128)(2,1)} %all-gather.5.cloned.1.call-done), kind=kLoop, calls=%fused_computation.129 | loop fusion | bytes 16777216 | tf_op jit(solution)/shard_map/slice | solution.py:79
  262.3 2.3 fusion.17
  264.7 2.3 fusion.15
  267.6 0.6 copy-done.8
  268.2 2.3 fusion.25
  270.6 2.3 fusion.23
  273.5 0.6 copy-done.7
  274.1 2.5 fusion.21
  276.7 2.3 fusion.19
  279.6 0.6 copy-done.6
  280.2 2.3 fusion.13
  282.5 2.3 fusion.11
  285.5 2.5 fusion.5
  288.0 2.8 fusion.9
  290.7 2.5 fusion.7
  293.3 6.8 %select_convert_fusion = bf16[64,128,128]{2,1,0:T(8,128)(2,1)} fusion(f32[64,128,128]{2,1,0:T(8,128)S(1)} %fusion.5, f32[64,128,128]{2,1,0:T(8,128)S(1)} %fusion.9, f32[64,128,128]{2,1,0:T(8,128)S(1)} %fusion.7, bf16[128,64,128]{2,1,0:T(8,128)(2,1)S(1)} %fusion.3, pred[64,128]{1,0:T(8,128)(4,1)S(1)} %broadcast_compare_fusion, ...), kind=kOutput, calls=%fused_computation.8 | convolution fusion | flops 274792448 | bytes 16818176 | tf_op jit(solution)/shard_map/dot_general | solution.py:57
  (42 shorter events, 4.8 us)
Async XLA Ops:
  6.5 116.1 %all-gather.3.cloned.1.call-start = ((), (), s32[]{:S(2)}) async-start(), calls=%async_computation | async-start | bytes 4456448 | tf_op jit(solution)/shard_map/all_gather | solution.py:67
  10.9 0.8 copy-start.10
  12.7 244.9 %all-gather.5.cloned.1.call-start = ((), (), s32[]{:S(2)}) async-start(), calls=%async_computation.1 | async-start | bytes 8650752 | tf_op jit(solution)/shard_map/all_gather | solution.py:68
  135.2 2.7 copy-start
  257.6 4.7 %copy-start.9 = (bf16[64,64,128]{2,0,1:T(8,128)(2,1)S(1)}, bf16[64,64,128]{2,0,1:T(8,128)(2,1)}, u32[]{:S(2)}) copy-start(bf16[64,64,128]{2,0,1:T(8,128)(2,1)} %get-tuple-element.10) | copy-start | bytes 3145732
  262.3 2.4 copy-start.3
  262.3 2.4 copy-start.5
  267.0 1.2 copy-start.8
  268.2 2.3 copy-start.1
  268.2 2.3 copy-start.4
  272.9 1.2 copy-start.7
  274.1 2.5 copy-start.2
  279.0 1.2 copy-start.6
Sparse Core Ops, SparseCore 0:
  12.8 109.7 all-gather.2
  125.9 131.6 all-gather.4
where the time goes:
time: 311 us; the launch traced here: 307 us
  waiting for transfers between devices  226 us (73%)
  matrix products  34.8 us (11%)
  local copies, waits for them, and re-layouts  19.6 us (6%)
  between operations  13.9 us (4%)
  other arithmetic  12.6 us (4%)
    all_gather x1, waiting for transfers between devices, on_device(): second = lax.all_gather(white, 'row', axis=1, tiled=True)  117 us
    all_gather x1, waiting for transfers between devices, on_device(): first = lax.all_gather(white, 'col', axis=1, tiled=True)  108 us
    dot_general x4, matrix products, lag_block(): lax.dot_general(stacked, table, (((0,), (0,)), ((), ())), preferred_eleme...  14.6 us
    dot_general x4, matrix products, cross_terms(): jnp.einsum('fik,fjk->fij', first, second, preferred_element_type=jnp.floa...  9.54 us
    dot_general x4, matrix products, cross_terms(): jnp.einsum('fik,fjk->fij', turned, second, preferred_element_type=jnp.flo...  9.29 us
    slice x2, local copies, waits for them, and re-layouts, on_device(): part_re, part_im = cross_terms(first[low:high], second[low:high])  7.4 us
    unnamed x26, local copies, waits for them, and re-layouts  6.67 us
  transfers between devices with their start and end apart: 2, of which 2 were waited for; matrix products, arithmetic and copies ran while one was open for 6% of the time, Pallas kernels for 0%

commit v1 on v0

--- a/solution.py
+++ b/solution.py
@@ -65,7 +65,9 @@
     per_dev = white.shape[1]
     width = F // 4
     first = lax.all_gather(white, "col", axis=1, tiled=True)
-    second = lax.all_gather(white, "row", axis=1, tiled=True)
+    second = jnp.concatenate(
+        lax.all_to_all(jnp.stack([white] * lax.axis_size("row")), "row", 0, 0), axis=1
+    )
     pairs = (first, second)
     rows = pairs[0].shape[1]
     cols = pairs[1].shape[1]

time: 311 us -> 409 us (1.32)
  the two profiles are of different devices: /device:TPU:1 before, /device:TPU:24 now
where the time goes in v1:
time: 409 us; the launch traced here: 404 us
  waiting for transfers between devices  301 us (74%)
  matrix products  34.7 us (8%)
  local copies, waits for them, and re-layouts  24.3 us (6%)
  starting transfers between devices  16.5 us (4%)
  between operations  14.1 us (3%)
  other arithmetic  12.6 us (3%)
    all_gather x1, waiting for transfers between devices, on_device(): first = lax.all_gather(white, 'col', axis=1, tiled=True)  301 us
    all_to_all x1, starting transfers between devices, on_device(): lax.all_to_all(jnp.stack([white] * lax.axis_size('row')), 'row', 0, 0)  16 us
    dot_general x4, matrix products, lag_block(): lax.dot_general(stacked, table, (((0,), (0,)), ((), ())), preferred_eleme...  14.6 us
    dot_general x4, matrix products, cross_terms(): jnp.einsum('fik,fjk->fij', first, second, preferred_element_type=jnp.floa...  9.54 us
    dot_general x4, matrix products, cross_terms(): jnp.einsum('fik,fjk->fij', turned, second, preferred_element_type=jnp.flo...  9.21 us
  transfers between devices with their start and end apart: 2, of which 1 were waited for; matrix products, arithmetic and copies ran while one was open for 5% of the time, Pallas kernels for 0%

profile of v1, /device:TPU:24, one launch (start us, length us, event | category | flops | bytes accessed | tf_op | source)
XLA Modules:
  0.0 403.5 jit_solution(5267969029552378314)
XLA Ops:
  6.6 2.1 sine_negate_fusion
  8.7 1.0 convert_multiply_fusion
  9.7 1.1 fusion.30
  12.0 5.3 %stack.2 = bf16[32,256,4,128]{3,1,2,0:T(8,128)(2,1)} broadcast(bf16[256,4,128]{2,0,1:T(8,128)(2,1)S(1)} %copy.37), dimensions={1,2,3} | broadcast | bytes 8650752 | tf_op jit(solution)/shard_map/stack | solution.py:69
  17.3 16.0 %all-to-all-start = ((bf16[32,256,4,128]{3,1,2,0:T(8,128)(2,1)}), bf16[32,256,4,128]{3,1,2,0:T(8,128)(2,1)}, u32[]{:S(2)}, u32[]{:S(2)}) async-start(bf16[32,256,4,128]{3,1,2,0:T(8,128)(2,1)} %stack.2), calls=%async_computation | async-start | bytes 16777216 | tf_op jit(solution)/shard_map/all_to_all | solution.py:69
  34.7 301.1 %all-gather.2.cloned.1.call-done = bf16[256,64,128]{2,0,1:T(8,128)(2,1)} async-done(((bf16[256,4,128]{2,0,1:T(8,128)(2,1)}), bf16[256,64,128]{2,0,1:T(8,128)(2,1)}) %all-gather.2.cloned.1.call-update) | async-done | bytes 4194320 | tf_op jit(solution)/shard_map/all_gather | solution.py:67
  335.8 4.3 %fusion.90 = (bf16[64,64,64]{2,0,1:T(8,128)(2,1)S(1)}, bf16[64,64,64]{2,0,1:T(8,128)(2,1)S(1)}, bf16[64,64,64]{2,0,1:T(8,128)(2,1)S(1)}, bf16[64,64,64]{2,0,1:T(...) fusion(bf16[256,64,128]{2,0,1:T(8,128)(2,1)} %all-gather.2.clon, ...), kind=kLoop, calls=%fused_computation.131 | loop fusion | bytes 8388608 | tf_op jit(solution)/shard_map/slice | solution.py:48
  340.2 1.7 copy.71
  341.9 1.7 copy.65
  343.6 0.7 copy.68
  344.2 0.7 copy.74
  344.9 1.8 copy_negate_fusion.1
  346.7 1.8 copy_negate_fusion.3
  348.5 1.8 copy_negate_fusion.2
  350.3 0.8 copy_negate_fusion
  351.1 2.6 fusion.89
  353.8 4.8 %fusion.88 = (bf16[64,32,4,128]{3,0,2,1:T(8,128)(2,1)S(1)}, bf16[64,32,4,128]{3,0,2,1:T(8,128)(2,1)S(1)}, bf16[64,32,4,128]{3,0,2,1:T(8,128)(2,1)S(1)}, bf16[64,32,4,128]{3,0,2,1:T(8,128)(2,1)S(1)}) fusion(bf16[256,32,4,128]{3,0,2,1:T(8,128)(2,1)} %bitcast.4), kind=kLoop, calls=%fused_computation.129 | loop fusion | bytes 16777216 | tf_op jit(solution)/shard_map/slice | solution.py:81
  358.6 2.3 fusion.17
  361.0 2.3 fusion.15
  363.8 0.6 copy-done.8
  364.5 2.3 fusion.25
  366.8 2.3 fusion.23
  369.7 0.6 copy-done.7
  370.3 2.5 fusion.21
  372.9 2.3 fusion.19
  375.8 0.6 copy-done.6
  376.4 2.3 fusion.13
  378.8 2.3 fusion.11
  381.7 2.5 fusion.5
  384.2 2.8 fusion.9
  386.9 2.5 fusion.7
  389.5 6.8 %select_convert_fusion = bf16[64,128,128]{2,1,0:T(8,128)(2,1)} fusion(f32[64,128,128]{2,1,0:T(8,128)S(1)} %fusion.5, f32[64,128,128]{2,1,0:T(8,128)S(1)} %fusion.9, f32[64,128,128]{2,1,0:T(8,128)S(1)} %fusion.7, bf16[128,64,128]{2,1,0:T(8,128)(2,1)S(1)} %fusion.3, pred[64,128]{1,0:T(8,128)(4,1)S(1)} %broadcast_compare_fusion, ...), kind=kOutput, calls=%fused_computation.8 | convolution fusion | flops 274792448 | bytes 16818176 | tf_op jit(solution)/shard_map/dot_general | solution.py:57
  (44 shorter events, 4.9 us)
Async XLA Ops:
  10.9 0.8 copy-start.11
  12.0 5.3 %copy-start.10 = (bf16[256,4,128]{2,0,1:T(8,128)(2,1)}, bf16[256,4,128]{2,0,1:T(8,128)(2,1)S(1)}, u32[]{:S(2)}) copy-start(bf16[256,4,128]{2,0,1:T(8,128)(2,1)S(1)} %copy.37) | copy-start | bytes 786436
  17.3 336.5 %all-to-all-start = ((bf16[32,256,4,128]{3,1,2,0:T(8,128)(2,1)}), bf16[32,256,4,128]{3,1,2,0:T(8,128)(2,1)}, u32[]{:S(2)}, u32[]{:S(2)}) async-start(bf16[32,256,4,128]{3,1,2,0:T(8,128)(2,1)} %stack.2), calls=%async_computation | async-start | bytes 16777216 | tf_op jit(solution)/shard_map/all_to_all | solution.py:69
  33.3 302.5 %all-gather.2.cloned.1.call-start = ((), (), s32[]{:S(2)}) async-start(), calls=%async_computation.1 | async-start | bytes 4456448 | tf_op jit(solution)/shard_map/all_gather | solution.py:67
  348.5 2.6 copy-start
  353.8 4.8 %copy-start.9 = (bf16[64,64,128]{2,0,1:T(8,128)(2,1)S(1)}, bf16[64,64,128]{2,0,1:T(8,128)(2,1)}, u32[]{:S(2)}) copy-start(bf16[64,64,128]{2,0,1:T(8,128)(2,1)} %get-tuple-element.10) | copy-start | bytes 3145732
  358.6 2.4 copy-start.3
  358.6 2.4 copy-start.5
  363.3 1.2 copy-start.8
  364.5 2.3 copy-start.1
  364.5 2.3 copy-start.4
  369.1 1.2 copy-start.7
  370.3 2.5 copy-start.2
  375.2 1.2 copy-start.6
Sparse Core Ops, SparseCore 0:
  36.2 299.5 all-gather.1
